TPU v7x, 32 devices: a whole 2x2x4 slice. The times are simulated.
32 devices in a mesh: ctx: 4 (over y, x), fsdp: 8 (over z, core).
Axes of the slice: x: 2, y: 2, z: 4, core: 2. Of those that a mesh axis runs over, the one named last changes fastest.
Arguments:
- tokens: bfloat16 [8, 512, 2048], P('fsdp', 'ctx'), may hold values from -6 to 6
- cotangent: bfloat16 [8, 512, 2048], P('fsdp', 'ctx'), may hold values from -6 to 6
- block_ids: int32 [8, 512], P('fsdp', 'ctx'), may hold values from 0 to 2, as said below
- span_order: int32 [8, 8], P('fsdp'), may hold values from 0 to 7, as said below
- attn_gain: bfloat16 [2048], P('fsdp'), may hold values from 0.099609375 to 1.8984375
- w_qkv: bfloat16 [2048, 3, 2048], P('fsdp'), may hold values from -0.125 to 0.125
- w_out: bfloat16 [2048, 2048], P('fsdp'), may hold values from -0.75 to 0.75
- ffn_gain: bfloat16 [2048], P('fsdp'), may hold values from 0.099609375 to 1.8984375
- w_gate_up: bfloat16 [2048, 2, 8192], P('fsdp'), may hold values from -0.125 to 0.125
- w_down: bfloat16 [8192, 2048], P('fsdp'), may hold values from -0.0625 to 0.0625
Outputs:
- layer_out: bfloat16 [8, 512, 2048], P('fsdp', 'ctx')
- input_grad: bfloat16 [8, 512, 2048], P('fsdp', 'ctx')
- grad_attn_gain: float32 [2048], P('fsdp')
- grad_qkv: float32 [2048, 3, 2048], P('fsdp')
- grad_out: float32 [2048, 2048], P('fsdp')
- grad_ffn_gain: float32 [2048], P('fsdp')
- grad_gate_up: float32 [2048, 2, 8192], P('fsdp')
- grad_down: float32 [8192, 2048], P('fsdp')
Inputs may be any that keep to these rules, and one draw needn't show every extreme that they name: Each row is an ordering of 0 to 7; stored row i of a sequence holds position span_order[s, i // 64] * 64 + i % 64. `block_ids`: in order of positions the block numbers of a sequence start at 0, never fall and rise by one at a time; every sequence has exactly 3 blocks, each covering 1 to 256 consecutive positions, and one block of every sequence covers exactly 256.
All inputs are finite; a program needn't handle non-finite values.
Results may differ from a plain program's by a relative error of at most 0.023.
Values may be sent and summed in bfloat16 or wider, within the bound.
No kernel may reach another device: no remote copies, remote signals or barrier semaphores. Data moves between devices by JAX's collectives and lax.ppermute only.
A program may use at most 576 MiB of HBM per device.

v0:
```python
import jax
import jax.numpy as jnp
from jax import lax
from jax.sharding import PartitionSpec as P

HD = 64
rope_theta = 130000.0
norm_eps = 1e-05
score_scale = 0.125
masked_score = -1e30


def shifted(array, axis, by):
    size = lax.axis_size(axis)
    return lax.ppermute(array, axis, [(i, (i + by) % size) for i in range(size)])


def angles(positions, width):
    half_width = width // 2
    frequency = rope_theta ** (-2.0 * jnp.arange(half_width, dtype=jnp.float32) / width)
    phases = positions.astype(jnp.float32)[:, None] * frequency[None, :]
    return (jnp.cos(phases)[:, None, :], jnp.sin(phases)[:, None, :])


def rotate(values, cosine, sine):
    half_width = values.shape[-1] // 2
    leading = values[..., :half_width]
    trailing = values[..., half_width:]
    return jnp.concatenate(
        [leading * cosine - trailing * sine, trailing * cosine + leading * sine], -1
    )


def inverse_rms(values):
    return lax.rsqrt(jnp.mean(values * values, -1, keepdims=True) + norm_eps)


def norm_back(grad_normed, normed, gain, inverse):
    scaled = grad_normed * gain
    return inverse * (scaled - normed * jnp.mean(scaled * normed, -1, keepdims=True))


def contract_rows(picked, right):
    return lax.dot_general(
        picked, right, (((0,), (0,)), ((), ())), preferred_element_type=jnp.float32
    )


def sectioned_rows(left, right):
    return lax.psum_scatter(
        contract_rows(left, right).astype(jnp.bfloat16), "fsdp", scatter_dimension=0, tiled=True
    ).astype(jnp.float32)


def per_device(
    tokens, cotangent, block_ids, span_order, attn_gain, w_qkv, w_out, ffn_gain, w_gate_up, w_down
):
    local_rows = tokens.shape[1]
    width = tokens.shape[2]
    heads = width // HD
    ctx_count = lax.axis_size("ctx")
    inputs = tokens[0].astype(jnp.float32)
    query_blocks = block_ids[0]
    half_rows = local_rows // 2
    row_ids = jnp.arange(local_rows, dtype=jnp.int32)
    slots = 2 * lax.axis_index("ctx") + row_ids // half_rows
    order_row = span_order[0]
    matches = slots[:, None] == jnp.arange(order_row.shape[0], dtype=jnp.int32)[None, :]
    picked = jnp.sum(jnp.where(matches, order_row[None, :], 0), axis=1)
    positions = picked * half_rows + row_ids % half_rows
    cosine, sine = angles(positions, HD)
    inverse_one = inverse_rms(inputs)
    normed_one = inputs * inverse_one
    gain_one, qkv_full, out_full = (
        lax.all_gather(attn_gain, "fsdp", axis=0, tiled=True),
        lax.all_gather(w_qkv, "fsdp", axis=0, tiled=True),
        lax.all_gather(w_out, "fsdp", axis=0, tiled=True),
    )
    gain_one = gain_one.astype(jnp.float32)
    act_one = (normed_one * gain_one).astype(jnp.bfloat16)
    qkv = jnp.einsum("td,dke->tke", act_one, qkv_full, preferred_element_type=jnp.float32)
    query = rotate(qkv[:, 0].reshape(local_rows, heads, HD), cosine, sine).astype(jnp.bfloat16)
    key_own = rotate(qkv[:, 1].reshape(local_rows, heads, HD), cosine, sine).astype(jnp.bfloat16)
    value_own = qkv[:, 2].reshape(local_rows, heads, HD).astype(jnp.bfloat16)
    all_blocks = lax.all_gather(query_blocks, "ctx", axis=0, tiled=True)

    def visible(start, count):
        key_blocks = lax.dynamic_slice_in_dim(all_blocks, start, count)
        return key_blocks[None, None, :] <= query_blocks[:, None, None]

    running_top = jnp.full((local_rows, heads), masked_score, jnp.float32)
    key_part = lax.all_gather(key_own, "ctx", axis=0, tiled=True)
    value_part = lax.all_gather(value_own, "ctx", axis=0, tiled=True)
    allowed = visible(jnp.int32(0), key_part.shape[0])
    scores = (
        jnp.einsum("qhe,khe->qhk", query, key_part, preferred_element_type=jnp.float32)
        * score_scale
    )
    scores = jnp.where(allowed, scores, masked_score)
    new_top = jnp.maximum(running_top, jnp.max(scores, -1))
    weights = jnp.where(allowed, jnp.exp(scores - new_top[..., None]), 0.0)
    accum = jnp.einsum(
        "qhk,khe->qhe", weights.astype(jnp.bfloat16), value_part, preferred_element_type=jnp.float32
    )
    running_top, running_total, accum = (new_top, jnp.sum(weights, -1), accum)
    attended = accum / running_total[..., None]
    log_total = running_top + jnp.log(running_total)
    attn_b = attended.reshape(local_rows, width).astype(jnp.bfloat16)
    resid = inputs + jnp.dot(attn_b, out_full, preferred_element_type=jnp.float32)
    inverse_two = inverse_rms(resid)
    normed_two = resid * inverse_two
    gain_two, gate_up_full, down_full = (
        lax.all_gather(ffn_gain, "fsdp", axis=0, tiled=True),
        lax.all_gather(w_gate_up, "fsdp", axis=0, tiled=True),
        lax.all_gather(w_down, "fsdp", axis=0, tiled=True),
    )
    gain_two = gain_two.astype(jnp.float32)
    act_two = (normed_two * gain_two).astype(jnp.bfloat16)
    gate_up = jnp.einsum("td,dkf->tkf", act_two, gate_up_full, preferred_element_type=jnp.float32)
    gate = gate_up[:, 0]
    upward = gate_up[:, 1]
    sigma = jax.nn.sigmoid(gate)
    swish = gate * sigma
    hidden = (swish * upward).astype(jnp.bfloat16)
    output = resid + jnp.dot(hidden, down_full, preferred_element_type=jnp.float32)
    layer_out = output.astype(jnp.bfloat16)[None]
    grad_out_rows = cotangent[0]
    grad_hidden = lax.dot_general(
        grad_out_rows, down_full, (((1,), (1,)), ((), ())), preferred_element_type=jnp.float32
    )
    grad_gate = grad_hidden * upward * sigma * (1.0 + gate * (1.0 - sigma))
    grad_up = grad_hidden * swish
    grad_gu = jnp.stack([grad_gate, grad_up], 1).astype(jnp.bfloat16)
    grad_act_two = jnp.einsum(
        "tkf,dkf->td", grad_gu, gate_up_full, preferred_element_type=jnp.float32
    )
    grad_gain_two = jnp.sum(grad_act_two * normed_two, 0)
    grad_resid = grad_out_rows.astype(jnp.float32) + norm_back(
        grad_act_two, normed_two, gain_two, inverse_two
    )
    grad_branch = grad_resid.astype(jnp.bfloat16)
    grad_attended = lax.dot_general(
        grad_branch, out_full, (((1,), (1,)), ((), ())), preferred_element_type=jnp.float32
    )
    grad_attended = grad_attended.astype(jnp.bfloat16).reshape(local_rows, heads, HD)
    delta = jnp.sum(grad_attended.astype(jnp.float32) * attended, -1)

    def key_terms(key_part, value_part, start):
        allowed = visible(start, key_part.shape[0])
        scores = (
            jnp.einsum("qhe,khe->qhk", query, key_part, preferred_element_type=jnp.float32)
            * score_scale
        )
        probs = jnp.where(allowed, jnp.exp(scores - log_total[..., None]), 0.0)
        grad_value = jnp.einsum(
            "qhk,qhe->khe",
            probs.astype(jnp.bfloat16),
            grad_attended,
            preferred_element_type=jnp.float32,
        )
        grad_probs = jnp.einsum(
            "qhe,khe->qhk", grad_attended, value_part, preferred_element_type=jnp.float32
        )
        grad_scores = (probs * (grad_probs - delta[..., None])).astype(jnp.bfloat16)
        grad_query = (
            jnp.einsum("qhk,khe->qhe", grad_scores, key_part, preferred_element_type=jnp.float32)
            * score_scale
        )
        grad_key = (
            jnp.einsum("qhk,qhe->khe", grad_scores, query, preferred_element_type=jnp.float32)
            * score_scale
        )
        return (grad_query, grad_key, grad_value)

    def pass_step(step, carry):
        key_part, value_part, grad_key, grad_value, grad_query = carry
        owner = (lax.axis_index("ctx") - step) % ctx_count
        query_add, key_add, value_add = key_terms(key_part, value_part, owner * local_rows)
        key_part, value_part = shifted((key_part, value_part), "ctx", 1)
        grad_key, grad_value = (
            shifted((grad_key + key_add).astype(jnp.bfloat16), "ctx", 1).astype(jnp.float32),
            shifted((grad_value + value_add).astype(jnp.bfloat16), "ctx", 1).astype(jnp.float32),
        )
        return (key_part, value_part, grad_key, grad_value, grad_query + query_add)

    empty = jnp.zeros((local_rows, heads, HD), jnp.float32)
    final = lax.fori_loop(0, ctx_count, pass_step, (key_own, value_own, empty, empty, empty))
    grad_query, grad_key, grad_value = (final[4], final[2], final[3])
    grad_qkv_rows = jnp.stack(
        [
            rotate(grad_query, cosine, -sine).reshape(local_rows, width),
            rotate(grad_key, cosine, -sine).reshape(local_rows, width),
            grad_value.reshape(local_rows, width),
        ],
        1,
    ).astype(jnp.bfloat16)
    grad_act_one = jnp.einsum(
        "tke,dke->td", grad_qkv_rows, qkv_full, preferred_element_type=jnp.float32
    )
    grad_gain_one = jnp.sum(grad_act_one * normed_one, 0)
    grad_inputs = grad_resid + norm_back(grad_act_one, normed_one, gain_one, inverse_one)
    input_grad = grad_inputs.astype(jnp.bfloat16)[None]
    part_qkv = sectioned_rows(act_one, grad_qkv_rows)
    part_out = sectioned_rows(attn_b, grad_branch)
    part_gate_up = sectioned_rows(act_two, grad_gu)
    part_down = sectioned_rows(hidden, grad_out_rows)
    gain_parts = (
        lax.psum_scatter(grad_gain_one, "fsdp", scatter_dimension=0, tiled=True),
        lax.psum_scatter(grad_gain_two, "fsdp", scatter_dimension=0, tiled=True),
    )
    summed = (
        lax.psum(gain_parts[0].astype(jnp.bfloat16), "ctx").astype(jnp.float32),
        lax.psum(part_qkv.astype(jnp.bfloat16), "ctx").astype(jnp.float32),
        lax.psum(part_out.astype(jnp.bfloat16), "ctx").astype(jnp.float32),
        lax.psum(gain_parts[1].astype(jnp.bfloat16), "ctx").astype(jnp.float32),
        lax.psum(part_gate_up.astype(jnp.bfloat16), "ctx").astype(jnp.float32),
        lax.psum(part_down.astype(jnp.bfloat16), "ctx").astype(jnp.float32),
    )
    return (layer_out, input_grad, summed[0], summed[1], summed[2], summed[3], summed[4], summed[5])


def solution(mesh):
    return jax.shard_map(
        per_device,
        mesh=mesh,
        in_specs=(
            P("fsdp", "ctx", None),
            P("fsdp", "ctx", None),
            P("fsdp", "ctx"),
            P("fsdp", None),
            P("fsdp"),
            P("fsdp", None, None),
            P("fsdp", None),
            P("fsdp"),
            P("fsdp", None, None),
            P("fsdp", None),
        ),
        out_specs=(
            P("fsdp", "ctx", None),
            P("fsdp", "ctx", None),
            P("fsdp"),
            P("fsdp", None, None),
            P("fsdp", None),
            P("fsdp"),
            P("fsdp", None, None),
            P("fsdp", None),
        ),
        check_vma=False,
    )
```

profile of v0, /device:TPU:0, one launch (start us, length us, event | category | flops | bytes accessed | tf_op | source)
XLA Modules:
  0.0 3121.4 jit_solution(10979373377277663653)
XLA Ops:
  8.6 13.4 all-gather.1
  24.9 207.3 %all-gather.10.cloned.1.call-done = bf16[2048,3,2048]{2,0,1:T(8,128)(2,1)} async-done(((bf16[256,3,2048]{2,0,1:T(8,128)(2,1)}), bf16[2048,3,2048]{2,0,1:T(8,128)(2,1)}) %all-gather.10.cloned.1.call-update) | async-done | bytes 25165840 | tf_op jit(solution)/shard_map/all_gather | solution.py:76
  232.2 10.2 fusion.61
  243.9 2.5 copy.71
  246.4 2.5 copy.70
  249.0 2.5 subtract_convert_fusion.2
  255.9 13.1 copy.73
  269.8 8.7 all-gather.2
  278.5 8.0 all-gather
  286.7 3.4 fusion.12
  290.1 3.4 copy-done.1
  295.5 27.4 all-gather.12.cloned.1.call-done
  322.9 7.4 fusion.81
  330.4 76.1 %all-gather.16.cloned.1.call-done = bf16[2048,2048]{1,0:T(8,128)(2,1)} async-done(((bf16[256,2048]{1,0:T(8,128)(2,1)}), bf16[2048,2048]{1,0:T(8,128)(2,1)}) %all-gather.16.cloned.1.call-update) | async-done | bytes 8388624 | tf_op jit(solution)/shard_map/all_gather | solution.py:77
  406.5 4.7 multiply_reduce_fusion.3
  411.2 559.8 %all-gather.18.cloned.1.call-done = bf16[2048,2,8192]{2,0,1:T(8,128)(2,1)} async-done(((bf16[256,2,8192]{2,0,1:T(8,128)(2,1)}), bf16[2048,2,8192]{2,0,1:T(8,128)(2,1)}) %all-gather.18.cloned.1.call-update) | async-done | bytes 67108880 | tf_op jit(solution)/shard_map/all_gather | solution.py:114
  971.1 31.7 %fusion.64 = f32[128,2,8192]{2,0,1:T(8,128)} fusion(bf16[2048,2,8192]{2,0,1:T(8,128)(2,1)} %all-gather.18.cloned.1.call-done, f32[128,2048]{1,0:T(8,128)S(1)} %get-tuple-element.443, f32[2048]{0:T(1024)S(1)} %bitcast.209, f32[128]{0:T(128)S(1)} %add_rsqrt_fusion), kind=kOutput, calls=%fused_computation.105 | convolution fusion | flops 8590721024 | bytes 76554752 | tf_op jit(solution)/shard_map/td,dkf->tkf/dot_general | solution.py:119
  1002.8 256.6 %all-gather.20.cloned.1.call-done = bf16[8192,2048]{1,0:T(8,128)(2,1)} async-done(((bf16[1024,2048]{1,0:T(8,128)(2,1)}), bf16[8192,2048]{1,0:T(8,128)(2,1)}) %all-gather.20.cloned.1.call-update) | async-done | bytes 33554448 | tf_op jit(solution)/shard_map/all_gather | solution.py:115
  1259.4 19.2 fusion.33
  1278.5 30.5 multiply_reduce_fusion
  1310.8 5.7 convolution_convert_fusion.3
  1318.3 7.1 convolution_convert_fusion.4
  1327.1 217.1 %while.24 = (s32[]{:T(128)}, bf16[128,32,64]{0,2,1:T(8,128)(2,1)S(1)}, bf16[128,32,64]{0,2,1:T(8,128)(2,1)}, f32[128,32,64]{0,2,1:T(8,128)}, f32[128,32,64]{0,2,...) while((s32[]{:T(128)}, ...), condition=%wide.region_8.9_spmd.clone, body=%wide.region_7.8_spmd.clone.sunk | while | flops 342376448 | bytes 36244028 | solution.py:187
  1330.9 2.7 fusion.135
  1341.6 7.9 collective-permute-done.2
  1351.7 9.1 collective-permute-done.3
  1362.9 9.0 collective-permute-done
  1371.9 10.7 collective-permute-done.1
  1386.1 3.0 fusion.135
  1391.3 2.4 collective-permute-start.3
  1395.8 2.6 fusion.137
  1398.4 6.8 collective-permute-done.2
  1407.4 9.1 collective-permute-done.3
  1418.6 9.0 collective-permute-done
  1427.6 9.8 collective-permute-done.1
  1440.9 3.0 fusion.135
  1445.6 2.9 collective-permute-start.3
  1450.6 2.6 fusion.137
  1453.2 6.8 collective-permute-done.2
  1462.1 9.1 collective-permute-done.3
  1473.4 9.0 collective-permute-done
  1482.4 8.9 collective-permute-done.1
  1494.8 3.0 fusion.135
  1499.5 3.0 collective-permute-start.3
  1504.4 2.6 fusion.137
  1507.0 6.8 collective-permute-done.2
  1516.0 9.1 collective-permute-done.3
  1527.3 9.0 collective-permute-done
  1536.2 8.0 collective-permute-done.1
  1548.2 11.9 convolution_convert_fusion.2
  1561.1 18.5 convolution_convert_fusion.1
  1580.9 28.3 convolution_convert_fusion
  1609.3 195.6 %reduce-scatter.5.cloned.1.call-done = bf16[256,3,2048]{2,0,1:T(8,128)(2,1)} async-done(((bf16[2048,3,2048]{2,0,1:T(8,128)(2,1)}), bf16[256,3,2048]{2,0,1:T(8,128)(2,1)}) %reduce-scatter.5.cloned.1.call-update) | async-done | bytes 3145744 | tf_op jit(solution)/shard_map/reduce_scatter | solution.py:50
  1804.8 326.3 %reduce-scatter.11.cloned.1.call-done = bf16[1024,2048]{1,0:T(8,128)(2,1)} async-done(((bf16[8192,2048]{1,0:T(8,128)(2,1)}), bf16[1024,2048]{1,0:T(8,128)(2,1)}) %reduce-scatter.11.cloned.1.call-update) | async-done | bytes 4194320 | tf_op jit(solution)/shard_map/reduce_scatter | solution.py:50
  2131.1 640.8 %reduce-scatter.9.cloned.1.call-done = bf16[256,2,8192]{2,0,1:T(8,128)(2,1)} async-done(((bf16[2048,2,8192]{2,0,1:T(8,128)(2,1)}), bf16[256,2,8192]{2,0,1:T(8,128)(2,1)}) %reduce-scatter.9.cloned.1.call-update) | async-done | bytes 8388624 | tf_op jit(solution)/shard_map/reduce_scatter | solution.py:50
  2773.8 14.8 fusion.47
  2788.6 25.9 all-reduce.2
  2814.7 10.2 all-reduce.3
  2826.0 2.4 fusion.53
  2828.4 19.9 fusion.29
  2848.3 236.2 %all-reduce.7.cloned.1.call-done = (bf16[256,2,8192]{2,0,1:T(8,128)(2,1)}, bf16[256,3,2048]{2,0,1:T(8,128)(2,1)}, bf16[256,2048]{1,0:T(8,128)(2,1)}, bf16[1024,2048]{1,0:T(8,128)(2,1)}) async-done(((bf16[256,2,8192]{2,0,1:T(8,128)(2,1)}, bf16[256,3,2048]{2,0,1:T(8,128)(2,1)}, bf16[256,2048]{1,0:T(8,128)(2,1)}, bf16[1024,2048]{1,0:T(8,128)(2,1)}), (bf16[256,2,8192]{2,0,1:T(8,128)(2,1)}, ...) | async-done | bytes 16777232 | tf_op jit(solution)/shard_map/psum | solution.py:216
  3084.6 5.9 convert_element_type.193
  3092.0 18.2 copy.80
  3110.2 4.4 convert_element_type.203
  (168 shorter events, 79.3 us)
Async XLA Ops:
  7.2 225.0 %all-gather.10.cloned.1.call-start = ((), (), s32[]{:S(2)}) async-start(), calls=%async_computation.4 | async-start | bytes 28311552 | tf_op jit(solution)/shard_map/all_gather | solution.py:76
  7.9 278.7 %all-gather.14.cloned.1.call-start = ((), (), s32[]{:S(2)}) async-start(), calls=%async_computation.6 | async-start | bytes 2621440 | tf_op jit(solution)/shard_map/all_gather | solution.py:92
  252.3 70.6 %all-gather.12.cloned.1.call-start = ((), (), s32[]{:S(2)}) async-start(), calls=%async_computation.5 | async-start | bytes 2621440 | tf_op jit(solution)/shard_map/all_gather | solution.py:93
  255.3 151.1 %all-gather.16.cloned.1.call-start = ((), (), s32[]{:S(2)}) async-start(), calls=%async_computation.7 | async-start | bytes 9437184 | tf_op jit(solution)/shard_map/all_gather | solution.py:77
  255.9 715.2 %all-gather.18.cloned.1.call-start = ((), (), s32[]{:S(2)}) async-start(), calls=%async_computation.8 | async-start | bytes 75497472 | tf_op jit(solution)/shard_map/all_gather | solution.py:114
  269.1 0.7 copy-start.22
  269.1 9.3 copy-start.21
  269.1 17.5 copy-start.14
  269.1 990.2 %all-gather.20.cloned.1.call-start = ((), (), s32[]{:S(2)}) async-start(), calls=%async_computation.9 | async-start | bytes 37748736 | tf_op jit(solution)/shard_map/all_gather | solution.py:115
  269.7 1339.5 %reduce-scatter.7.cloned.1.call-start = ((), (), s32[]{:S(2)}) async-start(), calls=%async_computation.11 | async-start | bytes 9437184 | tf_op jit(solution)/shard_map/reduce_scatter | solution.py:50
  290.0 3.4 copy-start.1
  295.5 111.0 %copy-start.7 = (bf16[1,128,2048]{2,1,0:T(8,128)(2,1)S(1)}, bf16[1,128,2048]{2,1,0:T(8,128)(2,1)}, u32[]{:S(2)}) copy-start(bf16[1,128,2048]{2,1,0:T(8,128)(2,1)} %param.12) | copy-start | bytes 1572868
  330.4 80.9 %copy-start.11 = (bf16[128,32,64]{0,2,1:T(8,128)(2,1)}, bf16[128,32,64]{0,2,1:T(8,128)(2,1)S(1)}, u32[]{:S(2)}) copy-start(bf16[128,32,64]{0,2,1:T(8,128)(2,1)S(1)} %get-tuple-element.440) | copy-start | bytes 1572868
  411.2 897.8 %copy-start.2 = (f32[128,2048]{1,0:T(8,128)}, f32[128,2048]{1,0:T(8,128)S(1)}, u32[]{:S(2)}) copy-start(f32[128,2048]{1,0:T(8,128)S(1)} %get-tuple-element.443) | copy-start | bytes 3145732
  1278.5 30.5 copy-start.10
  1309.0 1.8 copy-start.12
  1310.7 7.6 copy-start.5
  1316.5 0.9 copy-start.15
  1316.5 488.3 %reduce-scatter.5.cloned.1.call-start = ((), (), s32[]{:S(2)}) async-start(), calls=%async_computation.10 | async-start | bytes 28311552 | tf_op jit(solution)/shard_map/reduce_scatter | solution.py:50
  1318.3 8.8 copy-start.4
  1327.1 218.7 %copy-start.20 = (f32[128,32]{0,1:T(8,128)S(1)}, f32[128,32]{0,1:T(8,128)}, u32[]{:S(2)}) copy-start(f32[128,32]{0,1:T(8,128)} %get-tuple-element.435) | copy-start | bytes 49156
  1330.3 4.6 copy-start
  1333.6 16.0 collective-permute-start.2
  1336.6 24.2 collective-permute-start.3
  1338.0 33.9 %collective-permute-start = (bf16[128,32,64]{0,2,1:T(8,128)(2,1)S(1)}, bf16[128,32,64]{0,2,1:T(8,128)(2,1)S(1)}, u32[]{:S(2)}, u32[]{:S(2)}) collective-permute-start(bf16[128,32,64]{0,2,1:T(8,128)(2,1)S(1)} %copy.96), channel_id=1, source_target_pairs={{0,8},{8,16},{16,24},{24,0},{1,9},{9,17},{17,25},{25,1},{2,10},{10... | collective-permute-start | bytes 1572872 | tf_op jit(solution)/shard_map/while/body/eval_jaxpr/ppermute | solution.py:15
  1339.5 43.1 %collective-permute-start.1 = (bf16[128,32,64]{0,2,1:T(8,128)(2,1)S(1)}, bf16[128,32,64]{0,2,1:T(8,128)(2,1)}, u32[]{:S(2)}, u32[]{:S(2)}) collective-permute-start(bf16[128,32,64]{0,2,1:T(8,128)(2,1)S(1)} %copy.97), channel_id=1, source_target_pairs={{0,8},{8,16},{16,24},{24,0},{1,9},{9,17},{17,25},{25,1},{2,10},{10... | collective-permute-start | bytes 1572872 | tf_op jit(solution)/shard_map/while/body/eval_jaxpr/ppermute | solution.py:15
  1385.6 4.0 copy-start
  1389.2 16.1 collective-permute-start.2
  1391.3 25.2 collective-permute-start.3
  1393.6 34.0 %collective-permute-start = (bf16[128,32,64]{0,2,1:T(8,128)(2,1)S(1)}, bf16[128,32,64]{0,2,1:T(8,128)(2,1)S(1)}, u32[]{:S(2)}, u32[]{:S(2)}) collective-permute-start(bf16[128,32,64]{0,2,1:T(8,128)(2,1)S(1)} %copy.96), channel_id=1, source_target_pairs={{0,8},{8,16},{16,24},{24,0},{1,9},{9,17},{17,25},{25,1},{2,10},{10... | collective-permute-start | bytes 1572872 | tf_op jit(solution)/shard_map/while/body/eval_jaxpr/ppermute | solution.py:15
  1394.2 43.2 %collective-permute-start.1 = (bf16[128,32,64]{0,2,1:T(8,128)(2,1)S(1)}, bf16[128,32,64]{0,2,1:T(8,128)(2,1)}, u32[]{:S(2)}, u32[]{:S(2)}) collective-permute-start(bf16[128,32,64]{0,2,1:T(8,128)(2,1)S(1)} %copy.97), channel_id=1, source_target_pairs={{0,8},{8,16},{16,24},{24,0},{1,9},{9,17},{17,25},{25,1},{2,10},{10... | collective-permute-start | bytes 1572872 | tf_op jit(solution)/shard_map/while/body/eval_jaxpr/ppermute | solution.py:15
  1440.4 3.6 copy-start
  1443.9 16.1 collective-permute-start.2
  1445.6 25.6 collective-permute-start.3
  1448.5 33.9 %collective-permute-start = (bf16[128,32,64]{0,2,1:T(8,128)(2,1)S(1)}, bf16[128,32,64]{0,2,1:T(8,128)(2,1)S(1)}, u32[]{:S(2)}, u32[]{:S(2)}) collective-permute-start(bf16[128,32,64]{0,2,1:T(8,128)(2,1)S(1)} %copy.96), channel_id=1, source_target_pairs={{0,8},{8,16},{16,24},{24,0},{1,9},{9,17},{17,25},{25,1},{2,10},{10... | collective-permute-start | bytes 1572872 | tf_op jit(solution)/shard_map/while/body/eval_jaxpr/ppermute | solution.py:15
  1448.5 42.8 %collective-permute-start.1 = (bf16[128,32,64]{0,2,1:T(8,128)(2,1)S(1)}, bf16[128,32,64]{0,2,1:T(8,128)(2,1)}, u32[]{:S(2)}, u32[]{:S(2)}) collective-permute-start(bf16[128,32,64]{0,2,1:T(8,128)(2,1)S(1)} %copy.97), channel_id=1, source_target_pairs={{0,8},{8,16},{16,24},{24,0},{1,9},{9,17},{17,25},{25,1},{2,10},{10... | collective-permute-start | bytes 1572872 | tf_op jit(solution)/shard_map/while/body/eval_jaxpr/ppermute | solution.py:15
  1494.2 3.6 copy-start
  1497.8 16.1 collective-permute-start.2
  1499.5 25.6 collective-permute-start.3
  1502.5 33.8 %collective-permute-start = (bf16[128,32,64]{0,2,1:T(8,128)(2,1)S(1)}, bf16[128,32,64]{0,2,1:T(8,128)(2,1)S(1)}, u32[]{:S(2)}, u32[]{:S(2)}) collective-permute-start(bf16[128,32,64]{0,2,1:T(8,128)(2,1)S(1)} %copy.96), channel_id=1, source_target_pairs={{0,8},{8,16},{16,24},{24,0},{1,9},{9,17},{17,25},{25,1},{2,10},{10... | collective-permute-start | bytes 1572872 | tf_op jit(solution)/shard_map/while/body/eval_jaxpr/ppermute | solution.py:15
  1502.5 41.8 %collective-permute-start.1 = (bf16[128,32,64]{0,2,1:T(8,128)(2,1)S(1)}, bf16[128,32,64]{0,2,1:T(8,128)(2,1)}, u32[]{:S(2)}, u32[]{:S(2)}) collective-permute-start(bf16[128,32,64]{0,2,1:T(8,128)(2,1)S(1)} %copy.97), channel_id=1, source_target_pairs={{0,8},{8,16},{16,24},{24,0},{1,9},{9,17},{17,25},{25,1},{2,10},{10... | collective-permute-start | bytes 1572872 | tf_op jit(solution)/shard_map/while/body/eval_jaxpr/ppermute | solution.py:15
  1545.6 2.7 copy-start.8
  1548.0 12.1 copy-start.17
  1548.2 11.9 copy-start.18
  1560.1 1.0 copy-start.16
  1560.1 571.0 %reduce-scatter.11.cloned.1.call-start = ((), (), s32[]{:S(2)}) async-start(), calls=%async_computation.13 | async-start | bytes 37748736 | tf_op jit(solution)/shard_map/reduce_scatter | solution.py:50
  1579.7 1.2 copy-start.3
  1579.7 1192.3 %reduce-scatter.9.cloned.1.call-start = ((), (), s32[]{:S(2)}) async-start(), calls=%async_computation.12 | async-start | bytes 75497472 | tf_op jit(solution)/shard_map/reduce_scatter | solution.py:50
  1609.2 1475.4 %all-reduce.7.cloned.1.call-start = ((), (), s32[]{:S(2)}) async-start(), calls=%async_computation.14 | async-start | bytes 33554432 | tf_op jit(solution)/shard_map/psum | solution.py:216
  2771.9 0.7 copy-start.23
  2773.8 52.2 %copy-start.6 = (f32[128,2048]{1,0:T(8,128)S(1)}, f32[128,2048]{1,0:T(8,128)}, u32[]{:S(2)}) copy-start(f32[128,2048]{1,0:T(8,128)} %copy-done.5) | copy-start | bytes 3145732
  3084.6 5.9 copy-start.19
  3084.6 7.5 copy-start.9
  3092.0 18.2 copy-start.13
Sparse Core Ops, SparseCore 0:
  9.6 222.5 all-gather.9
  252.5 33.3 all-gather.13
  287.7 35.1 all-gather.11
  324.4 82.0 all-gather.15
  408.5 562.5 all-gather.17
  972.5 286.8 all-gather.19
  1316.6 87.8 reduce-scatter.6
  1560.2 244.5 reduce-scatter.4
  1807.2 323.8 reduce-scatter.10
  2133.4 638.4 reduce-scatter.8
  2776.0 308.5 all-reduce.6
where the time goes:
time: 3130 us; the launch traced here: 3120 us
  waiting for transfers between devices  2670 us (85%)
  matrix products  250 us (8%)
  blocking collectives  66.2 us (2%)
  local copies, waits for them, and re-layouts  54.7 us (2%)
  other arithmetic  48.7 us (2%)
    reduce_scatter x4, waiting for transfers between devices, sectioned_rows(): lax.psum_scatter(contract_rows(left, right).astype(jnp.bfloat16), 'fsdp',...  1160 us
    all_gather x1, waiting for transfers between devices, per_device(): lax.all_gather(w_gate_up, 'fsdp', axis=0, tiled=True)  560 us
    all_gather x1, waiting for transfers between devices, per_device(): lax.all_gather(w_down, 'fsdp', axis=0, tiled=True)  257 us
    psum x1, waiting for transfers between devices, per_device(): lax.psum(part_gate_up.astype(jnp.bfloat16), 'ctx').astype(jnp.float32)  236 us
    all_gather x1, waiting for transfers between devices, per_device(): lax.all_gather(w_qkv, 'fsdp', axis=0, tiled=True)  207 us
    ppermute x16, waiting for transfers between devices, shifted(): lax.ppermute(array, axis, [(i, (i + by) % size) for i in range(size)])  138 us
    all_gather x1, waiting for transfers between devices, per_device(): lax.all_gather(w_out, 'fsdp', axis=0, tiled=True)  76.1 us
    dot_general x4, matrix products, contract_rows(): lax.dot_general(picked, right, (((0,), (0,)), ((), ())), preferred_elemen...  64.4 us
  transfers between devices with their start and end apart: 27, of which 25 were waited for; matrix products, arithmetic and copies ran while one was open for 8% of the time, Pallas kernels for 0%

commit v1 on v0

--- a/solution.py
+++ b/solution.py
@@ -213,7 +213,9 @@
         lax.psum(part_qkv.astype(jnp.bfloat16), "ctx").astype(jnp.float32),
         lax.psum(part_out.astype(jnp.bfloat16), "ctx").astype(jnp.float32),
         lax.psum(gain_parts[1].astype(jnp.bfloat16), "ctx").astype(jnp.float32),
-        lax.psum(part_gate_up.astype(jnp.bfloat16), "ctx").astype(jnp.float32),
+        jnp.sum(lax.all_gather(part_gate_up.astype(jnp.bfloat16), "ctx"), axis=0).astype(
+            jnp.float32
+        ),
         lax.psum(part_down.astype(jnp.bfloat16), "ctx").astype(jnp.float32),
     )
     return (layer_out, input_grad, summed[0], summed[1], summed[2], summed[3], summed[4], summed[5])

time: 3130 us -> 3300 us (1.054)
  waiting for transfers between devices: 2670 us -> 2820 us
    all_gather x0 -> x1, waiting for transfers between devices: none -> 285 us  [per_device(): lax.all_gather(part_gate_up.astype(jnp.bfloat16), 'ctx')]
    psum x1, waiting for transfers between devices: 236 us -> 99.6 us  [per_device(): lax.psum(part_qkv.astype(jnp.bfloat16), 'ctx').astype(jnp.float32)]
  transfers between devices with their start and end apart: 27 -> 28, of which waited for: 25 -> 26; matrix products, arithmetic and copies ran while one was open for 8% -> 8% of each run, Pallas kernels for 0% -> 0%
where the time goes in v1:
time: 3300 us; the launch traced here: 3290 us
  waiting for transfers between devices  2820 us (85%)
  matrix products  249 us (8%)
  other arithmetic  67.4 us (2%)
  blocking collectives  66.3 us (2%)
  local copies, waits for them, and re-layouts  54.1 us (2%)
    reduce_scatter x4, waiting for transfers between devices, sectioned_rows(): lax.psum_scatter(contract_rows(left, right).astype(jnp.bfloat16), 'fsdp',...  1160 us
    all_gather x1, waiting for transfers between devices, per_device(): lax.all_gather(w_gate_up, 'fsdp', axis=0, tiled=True)  560 us
    all_gather x1, waiting for transfers between devices, per_device(): lax.all_gather(part_gate_up.astype(jnp.bfloat16), 'ctx')  285 us
    all_gather x1, waiting for transfers between devices, per_device(): lax.all_gather(w_down, 'fsdp', axis=0, tiled=True)  257 us
    all_gather x1, waiting for transfers between devices, per_device(): lax.all_gather(w_qkv, 'fsdp', axis=0, tiled=True)  207 us
    ppermute x16, waiting for transfers between devices, shifted(): lax.ppermute(array, axis, [(i, (i + by) % size) for i in range(size)])  138 us
    psum x1, waiting for transfers between devices, per_device(): lax.psum(part_qkv.astype(jnp.bfloat16), 'ctx').astype(jnp.float32)  99.6 us
    all_gather x1, waiting for transfers between devices, per_device(): lax.all_gather(w_out, 'fsdp', axis=0, tiled=True)  76.1 us
  transfers between devices with their start and end apart: 28, of which 26 were waited for; matrix products, arithmetic and copies ran while one was open for 8% of the time, Pallas kernels for 0%

profile of v1, /device:TPU:0, one launch (start us, length us, event | category | flops | bytes accessed | tf_op | source)
XLA Modules:
  0.0 3288.6 jit_solution(1451158825933615520)
XLA Ops:
  8.6 13.4 all-gather.2
  24.9 207.3 %all-gather.12.cloned.1.call-done = bf16[2048,3,2048]{2,0,1:T(8,128)(2,1)} async-done(((bf16[256,3,2048]{2,0,1:T(8,128)(2,1)}), bf16[2048,3,2048]{2,0,1:T(8,128)(2,1)}) %all-gather.12.cloned.1.call-update) | async-done | bytes 25165840 | tf_op jit(solution)/shard_map/all_gather | solution.py:76
  232.2 10.2 fusion.61
  243.9 2.5 copy.69
  246.4 2.5 copy.68
  249.0 2.5 subtract_convert_fusion.2
  255.9 13.1 copy.71
  269.8 8.6 all-gather.3
  278.4 8.1 all-gather
  286.7 3.4 fusion.12
  290.1 3.4 copy-done.1
  295.5 27.4 all-gather.14.cloned.1.call-done
  322.9 7.4 fusion.81
  330.3 76.1 %all-gather.18.cloned.1.call-done = bf16[2048,2048]{1,0:T(8,128)(2,1)} async-done(((bf16[256,2048]{1,0:T(8,128)(2,1)}), bf16[2048,2048]{1,0:T(8,128)(2,1)}) %all-gather.18.cloned.1.call-update) | async-done | bytes 8388624 | tf_op jit(solution)/shard_map/all_gather | solution.py:77
  406.5 4.7 multiply_reduce_fusion.3
  411.2 559.8 %all-gather.20.cloned.1.call-done = bf16[2048,2,8192]{2,0,1:T(8,128)(2,1)} async-done(((bf16[256,2,8192]{2,0,1:T(8,128)(2,1)}), bf16[2048,2,8192]{2,0,1:T(8,128)(2,1)}) %all-gather.20.cloned.1.call-update) | async-done | bytes 67108880 | tf_op jit(solution)/shard_map/all_gather | solution.py:114
  971.1 31.7 fusion.64
  1002.8 256.6 %all-gather.22.cloned.1.call-done = bf16[8192,2048]{1,0:T(8,128)(2,1)} async-done(((bf16[1024,2048]{1,0:T(8,128)(2,1)}), bf16[8192,2048]{1,0:T(8,128)(2,1)}) %all-gather.22.cloned.1.call-update) | async-done | bytes 33554448 | tf_op jit(solution)/shard_map/all_gather | solution.py:115
  1259.4 19.2 fusion.33
  1278.5 30.4 multiply_reduce_fusion
  1310.7 5.7 convolution_convert_fusion.3
  1318.2 7.1 convolution_convert_fusion.4
  1327.0 217.0 %while.24 = (s32[]{:T(128)}, bf16[128,32,64]{0,2,1:T(8,128)(2,1)S(1)}, bf16[128,32,64]{0,2,1:T(8,128)(2,1)}, f32[128,32,64]{0,2,1:T(8,128)}, f32[128,32,64]{0,2,...) while((s32[]{:T(128)}, ...), condition=%wide.region_8.9_spmd.clone, body=%wide.region_7.8_spmd.clone.sunk | while | flops 342376448 | bytes 36244028 | solution.py:187
  1330.7 2.7 fusion.135
  1341.4 7.9 collective-permute-done.2
  1351.5 9.1 collective-permute-done.3
  1362.8 9.0 collective-permute-done
  1371.7 10.7 collective-permute-done.1
  1385.9 3.0 fusion.135
  1395.6 2.7 fusion.137
  1398.2 6.8 collective-permute-done.2
  1407.2 9.1 collective-permute-done.3
  1418.4 9.0 collective-permute-done
  1427.4 9.8 collective-permute-done.1
  1440.7 3.0 fusion.135
  1445.4 2.9 collective-permute-start.3
  1450.4 2.6 fusion.137
  1453.0 6.8 collective-permute-done.2
  1461.9 9.1 collective-permute-done.3
  1473.2 9.0 collective-permute-done
  1482.2 8.9 collective-permute-done.1
  1494.6 3.0 fusion.135
  1499.3 3.0 collective-permute-start.3
  1504.2 2.6 fusion.137
  1506.8 6.8 collective-permute-done.2
  1515.8 9.1 collective-permute-done.3
  1527.1 9.0 collective-permute-done
  1536.0 8.0 collective-permute-done.1
  1548.0 12.0 convolution_convert_fusion.2
  1561.0 18.5 convolution_convert_fusion.1
  1580.7 28.2 convolution_convert_fusion
  1609.0 195.8 %reduce-scatter.5.cloned.1.call-done = bf16[256,3,2048]{2,0,1:T(8,128)(2,1)} async-done(((bf16[2048,3,2048]{2,0,1:T(8,128)(2,1)}), bf16[256,3,2048]{2,0,1:T(8,128)(2,1)}) %reduce-scatter.5.cloned.1.call-update) | async-done | bytes 3145744 | tf_op jit(solution)/shard_map/reduce_scatter | solution.py:50
  1804.7 326.3 %reduce-scatter.11.cloned.1.call-done = bf16[1024,2048]{1,0:T(8,128)(2,1)} async-done(((bf16[8192,2048]{1,0:T(8,128)(2,1)}), bf16[1024,2048]{1,0:T(8,128)(2,1)}) %reduce-scatter.11.cloned.1.call-update) | async-done | bytes 4194320 | tf_op jit(solution)/shard_map/reduce_scatter | solution.py:50
  2131.1 640.8 %reduce-scatter.9.cloned.1.call-done = bf16[256,2,8192]{2,0,1:T(8,128)(2,1)} async-done(((bf16[2048,2,8192]{2,0,1:T(8,128)(2,1)}), bf16[256,2,8192]{2,0,1:T(8,128)(2,1)}) %reduce-scatter.9.cloned.1.call-update) | async-done | bytes 8388624 | tf_op jit(solution)/shard_map/reduce_scatter | solution.py:50
  2773.8 14.6 fusion.47
  2788.4 25.9 all-reduce.2
  2814.5 10.3 all-reduce.3
  2828.3 19.7 fusion.29
  2848.0 99.6 %all-reduce.7.cloned.1.call-done = (bf16[256,3,2048]{2,0,1:T(8,128)(2,1)}, bf16[256,2048]{1,0:T(8,128)(2,1)}, bf16[1024,2048]{1,0:T(8,128)(2,1)}) async-done(((bf16[256,3,2048]{2,0,1:T(8,128)(2,1)}, bf16[256,2048]{1,0:T(8,128)(2,1)}, bf16[1024,2048]{1,0:T(8,128)(2,1)}), (bf16[256,3,2048]{2,0,1:T(8,128)(2,1)}, bf16[256,2048]{1,0:T(8,128)(2,1)}, bf16[1024,2048]{1,0:T(8,128)(2,1)})) %all-reduce.7.cloned.1.call-update) | async-done | bytes 8388624 | tf_op jit(solution)/shard_map/psum | solution.py:213
  2947.6 5.6 convert_element_type.195
  2954.7 7.2 convert_element_type.205
  2961.9 285.5 %all-gather.24.cloned.1.call-done = bf16[1024,2,8192]{2,0,1:T(8,128)(2,1)} async-done(((bf16[256,2,8192]{2,0,1:T(8,128)(2,1)}), bf16[1024,2,8192]{2,0,1:T(8,128)(2,1)}) %all-gather.24.cloned.1.call-update) | async-done | bytes 33554448 | tf_op jit(solution)/shard_map/all_gather | solution.py:216
  3247.4 16.3 reduce_sum.102
  3263.7 17.6 copy.78
  (170 shorter events, 84.1 us)
Async XLA Ops:
  7.2 225.0 %all-gather.12.cloned.1.call-start = ((), (), s32[]{:S(2)}) async-start(), calls=%async_computation.4 | async-start | bytes 28311552 | tf_op jit(solution)/shard_map/all_gather | solution.py:76
  7.9 278.8 %all-gather.16.cloned.1.call-start = ((), (), s32[]{:S(2)}) async-start(), calls=%async_computation.6 | async-start | bytes 2621440 | tf_op jit(solution)/shard_map/all_gather | solution.py:92
  252.3 70.6 %all-gather.14.cloned.1.call-start = ((), (), s32[]{:S(2)}) async-start(), calls=%async_computation.5 | async-start | bytes 2621440 | tf_op jit(solution)/shard_map/all_gather | solution.py:93
  255.3 151.2 %all-gather.18.cloned.1.call-start = ((), (), s32[]{:S(2)}) async-start(), calls=%async_computation.7 | async-start | bytes 9437184 | tf_op jit(solution)/shard_map/all_gather | solution.py:77
  255.9 715.2 %all-gather.20.cloned.1.call-start = ((), (), s32[]{:S(2)}) async-start(), calls=%async_computation.8 | async-start | bytes 75497472 | tf_op jit(solution)/shard_map/all_gather | solution.py:114
  269.1 0.7 copy-start.21
  269.1 9.3 copy-start.20
  269.1 17.6 copy-start.13
  269.1 990.2 %all-gather.22.cloned.1.call-start = ((), (), s32[]{:S(2)}) async-start(), calls=%async_computation.9 | async-start | bytes 37748736 | tf_op jit(solution)/shard_map/all_gather | solution.py:115
  269.7 1339.3 %reduce-scatter.7.cloned.1.call-start = ((), (), s32[]{:S(2)}) async-start(), calls=%async_computation.11 | async-start | bytes 9437184 | tf_op jit(solution)/shard_map/reduce_scatter | solution.py:50
  290.0 3.4 copy-start.1
  295.5 110.9 %copy-start.7 = (bf16[1,128,2048]{2,1,0:T(8,128)(2,1)S(1)}, bf16[1,128,2048]{2,1,0:T(8,128)(2,1)}, u32[]{:S(2)}) copy-start(bf16[1,128,2048]{2,1,0:T(8,128)(2,1)} %param.12) | copy-start | bytes 1572868
  330.3 80.9 %copy-start.10 = (bf16[128,32,64]{0,2,1:T(8,128)(2,1)}, bf16[128,32,64]{0,2,1:T(8,128)(2,1)S(1)}, u32[]{:S(2)}) copy-start(bf16[128,32,64]{0,2,1:T(8,128)(2,1)S(1)} %get-tuple-element.423) | copy-start | bytes 1572868
  411.2 897.7 %copy-start.2 = (f32[128,2048]{1,0:T(8,128)}, f32[128,2048]{1,0:T(8,128)S(1)}, u32[]{:S(2)}) copy-start(f32[128,2048]{1,0:T(8,128)S(1)} %get-tuple-element.426) | copy-start | bytes 3145732
  1278.5 30.4 copy-start.9
  1308.9 1.8 copy-start.11
  1310.6 7.6 copy-start.5
  1316.4 0.9 copy-start.14
  1316.4 488.3 %reduce-scatter.5.cloned.1.call-start = ((), (), s32[]{:S(2)}) async-start(), calls=%async_computation.10 | async-start | bytes 28311552 | tf_op jit(solution)/shard_map/reduce_scatter | solution.py:50
  1318.2 8.8 copy-start.4
  1327.0 218.6 %copy-start.19 = (f32[128,32]{0,1:T(8,128)S(1)}, f32[128,32]{0,1:T(8,128)}, u32[]{:S(2)}) copy-start(f32[128,32]{0,1:T(8,128)} %get-tuple-element.418) | copy-start | bytes 49156
  1330.2 4.5 copy-start
  1333.4 16.0 collective-permute-start.2
  1336.4 24.2 collective-permute-start.3
  1337.9 33.9 %collective-permute-start = (bf16[128,32,64]{0,2,1:T(8,128)(2,1)S(1)}, bf16[128,32,64]{0,2,1:T(8,128)(2,1)S(1)}, u32[]{:S(2)}, u32[]{:S(2)}) collective-permute-start(bf16[128,32,64]{0,2,1:T(8,128)(2,1)S(1)} %copy.94), channel_id=1, source_target_pairs={{0,8},{8,16},{16,24},{24,0},{1,9},{9,17},{17,25},{25,1},{2,10},{10... | collective-permute-start | bytes 1572872 | tf_op jit(solution)/shard_map/while/body/eval_jaxpr/ppermute | solution.py:15
  1339.3 43.1 %collective-permute-start.1 = (bf16[128,32,64]{0,2,1:T(8,128)(2,1)S(1)}, bf16[128,32,64]{0,2,1:T(8,128)(2,1)}, u32[]{:S(2)}, u32[]{:S(2)}) collective-permute-start(bf16[128,32,64]{0,2,1:T(8,128)(2,1)S(1)} %copy.95), channel_id=1, source_target_pairs={{0,8},{8,16},{16,24},{24,0},{1,9},{9,17},{17,25},{25,1},{2,10},{10... | collective-permute-start | bytes 1572872 | tf_op jit(solution)/shard_map/while/body/eval_jaxpr/ppermute | solution.py:15
  1385.4 4.1 copy-start
  1389.0 16.1 collective-permute-start.2
  1391.1 25.1 collective-permute-start.3
  1393.5 33.9 %collective-permute-start = (bf16[128,32,64]{0,2,1:T(8,128)(2,1)S(1)}, bf16[128,32,64]{0,2,1:T(8,128)(2,1)S(1)}, u32[]{:S(2)}, u32[]{:S(2)}) collective-permute-start(bf16[128,32,64]{0,2,1:T(8,128)(2,1)S(1)} %copy.94), channel_id=1, source_target_pairs={{0,8},{8,16},{16,24},{24,0},{1,9},{9,17},{17,25},{25,1},{2,10},{10... | collective-permute-start | bytes 1572872 | tf_op jit(solution)/shard_map/while/body/eval_jaxpr/ppermute | solution.py:15
  1394.0 43.2 %collective-permute-start.1 = (bf16[128,32,64]{0,2,1:T(8,128)(2,1)S(1)}, bf16[128,32,64]{0,2,1:T(8,128)(2,1)}, u32[]{:S(2)}, u32[]{:S(2)}) collective-permute-start(bf16[128,32,64]{0,2,1:T(8,128)(2,1)S(1)} %copy.95), channel_id=1, source_target_pairs={{0,8},{8,16},{16,24},{24,0},{1,9},{9,17},{17,25},{25,1},{2,10},{10... | collective-permute-start | bytes 1572872 | tf_op jit(solution)/shard_map/while/body/eval_jaxpr/ppermute | solution.py:15
  1440.2 3.6 copy-start
  1443.7 16.1 collective-permute-start.2
  1445.4 25.6 collective-permute-start.3
  1448.3 33.9 %collective-permute-start = (bf16[128,32,64]{0,2,1:T(8,128)(2,1)S(1)}, bf16[128,32,64]{0,2,1:T(8,128)(2,1)S(1)}, u32[]{:S(2)}, u32[]{:S(2)}) collective-permute-start(bf16[128,32,64]{0,2,1:T(8,128)(2,1)S(1)} %copy.94), channel_id=1, source_target_pairs={{0,8},{8,16},{16,24},{24,0},{1,9},{9,17},{17,25},{25,1},{2,10},{10... | collective-permute-start | bytes 1572872 | tf_op jit(solution)/shard_map/while/body/eval_jaxpr/ppermute | solution.py:15
  1448.4 42.7 %collective-permute-start.1 = (bf16[128,32,64]{0,2,1:T(8,128)(2,1)S(1)}, bf16[128,32,64]{0,2,1:T(8,128)(2,1)}, u32[]{:S(2)}, u32[]{:S(2)}) collective-permute-start(bf16[128,32,64]{0,2,1:T(8,128)(2,1)S(1)} %copy.95), channel_id=1, source_target_pairs={{0,8},{8,16},{16,24},{24,0},{1,9},{9,17},{17,25},{25,1},{2,10},{10... | collective-permute-start | bytes 1572872 | tf_op jit(solution)/shard_map/while/body/eval_jaxpr/ppermute | solution.py:15
  1494.0 3.6 copy-start
  1497.6 16.1 collective-permute-start.2
  1499.3 25.6 collective-permute-start.3
  1502.3 33.8 %collective-permute-start = (bf16[128,32,64]{0,2,1:T(8,128)(2,1)S(1)}, bf16[128,32,64]{0,2,1:T(8,128)(2,1)S(1)}, u32[]{:S(2)}, u32[]{:S(2)}) collective-permute-start(bf16[128,32,64]{0,2,1:T(8,128)(2,1)S(1)} %copy.94), channel_id=1, source_target_pairs={{0,8},{8,16},{16,24},{24,0},{1,9},{9,17},{17,25},{25,1},{2,10},{10... | collective-permute-start | bytes 1572872 | tf_op jit(solution)/shard_map/while/body/eval_jaxpr/ppermute | solution.py:15
  1502.3 41.7 %collective-permute-start.1 = (bf16[128,32,64]{0,2,1:T(8,128)(2,1)S(1)}, bf16[128,32,64]{0,2,1:T(8,128)(2,1)}, u32[]{:S(2)}, u32[]{:S(2)}) collective-permute-start(bf16[128,32,64]{0,2,1:T(8,128)(2,1)S(1)} %copy.95), channel_id=1, source_target_pairs={{0,8},{8,16},{16,24},{24,0},{1,9},{9,17},{17,25},{25,1},{2,10},{10... | collective-permute-start | bytes 1572872 | tf_op jit(solution)/shard_map/while/body/eval_jaxpr/ppermute | solution.py:15
  1545.3 2.7 copy-start.8
  1547.8 12.2 copy-start.16
  1548.0 12.0 copy-start.17
  1560.0 1.0 copy-start.15
  1560.0 571.0 %reduce-scatter.11.cloned.1.call-start = ((), (), s32[]{:S(2)}) async-start(), calls=%async_computation.13 | async-start | bytes 37748736 | tf_op jit(solution)/shard_map/reduce_scatter | solution.py:50
  1579.5 1.2 copy-start.3
  1579.5 1192.4 %reduce-scatter.9.cloned.1.call-start = ((), (), s32[]{:S(2)}) async-start(), calls=%async_computation.12 | async-start | bytes 75497472 | tf_op jit(solution)/shard_map/reduce_scatter | solution.py:50
  1608.9 1338.7 %all-reduce.7.cloned.1.call-start = ((), (), s32[]{:S(2)}) async-start(), calls=%async_computation.15 | async-start | bytes 16777216 | tf_op jit(solution)/shard_map/psum | solution.py:213
  2131.1 1116.3 %all-gather.24.cloned.1.call-start = ((), (), s32[]{:S(2)}) async-start(), calls=%async_computation.14 | async-start | bytes 41943040 | tf_op jit(solution)/shard_map/all_gather | solution.py:216
  2771.9 0.7 copy-start.22
  2773.8 52.1 %copy-start.6 = (f32[128,2048]{1,0:T(8,128)S(1)}, f32[128,2048]{1,0:T(8,128)}, u32[]{:S(2)}) copy-start(f32[128,2048]{1,0:T(8,128)} %copy-done.5) | copy-start | bytes 3145732
  2947.6 5.6 copy-start.18
  2947.6 7.2 copy-start.12
Sparse Core Ops, SparseCore 0:
  9.6 222.5 all-gather.11
  252.5 33.3 all-gather.15
  287.7 35.1 all-gather.13
  324.4 82.0 all-gather.17
  408.5 562.5 all-gather.19
  972.5 286.8 all-gather.21
  1316.5 87.7 reduce-scatter.6
  1560.1 244.5 reduce-scatter.4
  1807.1 323.8 reduce-scatter.10
  2133.4 638.4 reduce-scatter.8
  2775.8 171.6 all-reduce.6
  2949.4 297.8 all-gather.23
